TPU v7x, 32 devices: a whole 2x2x4 slice. The times are simulated.
32 devices in a mesh: lists: 4 (over y, x), points: 8 (over z, core).
Axes of the slice: x: 2, y: 2, z: 4, core: 2. Of those that a mesh axis runs over, the one named last changes fastest.
Arguments:
- child_centroids: float32 [1024, 768], P(('lists', 'points')), may hold values from -6 to 6
- child_sizes: int32 [1024], P(('lists', 'points')), may hold values from 1 to 256
- parent_of: int32 [1024], P(('lists', 'points')), may hold values from 0 to 511, as said below
- points: bfloat16 [49152, 768], P(('lists', 'points')), may hold values from -6 to 6
- assign: int32 [49152], P(('lists', 'points')), may hold values from 0 to 127
- codes: int32 [49152, 96], P(('lists', 'points')), may hold values from 0 to 255
- rotation: bfloat16 [768, 768], replicated, may hold values from -0.21875 to 0.21875
Outputs:
- merged_centroids: float32 [512, 768], P(('lists', 'points'))
- codeword_means: float32 [768, 256], replicated
Inputs may be any that keep to these rules, and one draw needn't show every extreme that they name: `parent_of`: every parent has exactly two children. Of the 32 children of one device, at most 16 have parents in one block of 128 consecutive parent numbers, and exactly 16 in some block.
All inputs are finite; a program needn't handle non-finite values.
Results may differ from a plain program's by a relative error of at most 0.0042.
Values may be sent and summed in bfloat16 or wider, within the bound.
No kernel may reach another device: no remote copies, remote signals or barrier semaphores. Data moves between devices by JAX's collectives and lax.ppermute only.
A program may use at most 64 MiB of HBM per device.

v0:
```python
import jax
import jax.numpy as jnp
from jax import lax
from jax.sharding import PartitionSpec as P

CODEWORDS = 256


def body(child_centroids, child_sizes, parent_of, points, assign, codes, rotation):
    columns = lax.axis_size("points")
    child_count = child_centroids.shape[0]
    feature_width = child_centroids.shape[1]
    owner_parents = columns * child_count // 2
    child_weight = child_sizes.astype(jnp.float32)
    weighted = child_weight[:, None] * child_centroids
    all_rows, all_mass, all_parent = (
        lax.all_gather(weighted, "lists", axis=0, tiled=True),
        lax.all_gather(child_weight, "lists", axis=0, tiled=True),
        lax.all_gather(parent_of.astype(jnp.float32), "lists", axis=0, tiled=True),
    )
    parent_whole = all_parent.astype(jnp.int32)
    first_parent = lax.axis_index("lists") * owner_parents
    owned_here = (parent_whole >= first_parent) & (parent_whole < first_parent + owner_parents)
    got_rows = jnp.where(owned_here[:, None], all_rows, 0.0)
    got_mass = jnp.where(owned_here, all_mass, 0.0)
    seg_target = jnp.where(owned_here, parent_whole - first_parent, 0)
    partial_sum = jax.ops.segment_sum(got_rows, seg_target, num_segments=owner_parents)
    partial_mass = jax.ops.segment_sum(got_mass, seg_target, num_segments=owner_parents)
    shard_rows = owner_parents // columns
    total_sum, total_mass = lax.psum((partial_sum, partial_mass), "points")
    merged_all = total_sum / total_mass[:, None]
    lowered = merged_all.astype(jnp.bfloat16)
    merged = lax.dynamic_slice_in_dim(
        merged_all, lax.axis_index("points") * shard_rows, shard_rows, 0
    )
    chosen = jnp.take(lowered, assign, axis=0)
    residual = (points.astype(jnp.float32) - chosen.astype(jnp.float32)).astype(jnp.bfloat16)
    rotated = jnp.dot(residual, rotation, preferred_element_type=jnp.float32).astype(jnp.bfloat16)
    point_count = points.shape[0]
    subspaces = codes.shape[1]
    sub_width = feature_width // subspaces
    block_rows = min(128, point_count)
    block_count = point_count // block_rows
    codeword_ids = jnp.arange(CODEWORDS, dtype=jnp.int32)

    def accumulate(carried, block_inputs):
        code_sums, code_counts = carried
        rot_blk, code_blk = block_inputs
        onehot = (code_blk[:, :, None] == codeword_ids[None, None, :]).astype(jnp.bfloat16)
        code_sums = code_sums + jnp.einsum(
            "pmd,pmk->mdk", rot_blk, onehot, preferred_element_type=jnp.float32
        )
        code_counts = code_counts + jnp.sum(onehot, axis=0, dtype=jnp.float32)
        return ((code_sums, code_counts), None)

    initial = (
        jnp.zeros((subspaces, sub_width, CODEWORDS), jnp.float32),
        jnp.zeros((subspaces, CODEWORDS), jnp.float32),
    )
    (code_sums, code_counts), _ = lax.scan(
        accumulate,
        initial,
        (
            rotated.reshape(block_count, block_rows, subspaces, sub_width),
            codes.reshape(block_count, block_rows, subspaces),
        ),
    )
    total_sums, total_counts = lax.psum(
        (code_sums.reshape(feature_width, CODEWORDS), code_counts), ("lists", "points")
    )
    means = total_sums.reshape(subspaces, sub_width, CODEWORDS) / (1.0 + total_counts[:, None, :])
    return (merged, means.reshape(feature_width, CODEWORDS))


def solution(mesh):
    in_specs = (
        P(("lists", "points"), None),
        P(("lists", "points")),
        P(("lists", "points")),
        P(("lists", "points"), None),
        P(("lists", "points")),
        P(("lists", "points"), None),
        P(),
    )
    out_specs = (P(("lists", "points"), None), P())
    return jax.shard_map(body, mesh=mesh, in_specs=in_specs, out_specs=out_specs, check_vma=False)
```

profile of v0, /device:TPU:0, one launch (start us, length us, event | category | flops | bytes accessed | tf_op | source)
XLA Modules:
  0.0 357.0 jit_solution(9061663071165604065)
XLA Ops:
  11.5 11.3 %all-reduce.3 = (f32[128]{0:T(128)S(1)}, f32[128]{0:T(128)S(1)}) all-reduce(f32[128]{0:T(128)S(1)} %convert_dynamic-update-slice_fusion, f32[128]{0:T(128)S(1)} %convert_dynamic-update-slice_fusion.1), channel_id=1, replica_groups=mesh['lists'=4,'points'=8] {'lists'}, use_global_device_ids=true, to_apply=%add | all-reduce | flops 256 | bytes 2048
  23.8 9.0 %all_gather.10 = f32[128,768]{1,0:T(8,128)S(1)} all-gather(f32[32,768]{1,0:T(8,128)S(1)} %broadcast_multiply_fusion), channel_id=1, replica_groups=mesh['lists'=4,'points'=8] {'lists'}, dimensions={0}, use_global_device_ids=true | all-gather | bytes 491520 | tf_op jit(solution)/shard_map/all_gather | solution.py:17
  36.5 13.8 %psum.29 = f32[128]{0:T(128)S(1)} all-reduce(f32[128]{0:T(128)S(1)} %scatter_custom_fusion.1), channel_id=1, replica_groups=mesh['lists'=4,'points'=8] {'points'}, use_global_device_ids=true, to_apply=%region_3.4 | all-reduce | flops 128 | bytes 1024 | tf_op jit(solution)/shard_map/psum | solution.py:30
  52.1 39.0 %all-reduce.7.cloned.1.call-done = f32[128,768]{1,0:T(8,128)} async-done(((f32[128,768]{1,0:T(8,128)}), f32[128,768]{1,0:T(8,128)}) %all-reduce.7.cloned.1.call-update) | async-done | bytes 393232 | tf_op jit(solution)/shard_map/psum | solution.py:30
  92.9 5.7 %gather_fusion = bf16[1536,768]{1,0:T(8,128)(2,1)} fusion(bf16[128,768]{1,0:T(8,128)(2,1)S(1)} %get-tuple-element.81, s32[2048]{0:T(1024)S(1)} %pad_clamp_fusion), kind=kCustom, calls=%fused_computation | custom fusion | bytes 4724736 | tf_op jit(solution)/shard_map/jit(_take)/gather | solution.py:36
  98.6 6.0 %convolution_convert_fusion = bf16[1536,768]{1,0:T(8,128)(2,1)} fusion(bf16[768,768]{1,0:T(8,128)(2,1)S(1)} %copy-done, bf16[1536,768]{1,0:T(8,128)(2,1)} %param.12, bf16[1536,768]{1,0:T(8,128)(2,1)} %gather_fusion, pred[1536]{0:T(1024)(128)(4,1)S(1)} %compare_and_fusion), kind=kOutput, calls=%fused_computation.16 | convolution fusion | flops 1819017216 | bytes 8259072 | tf_op jit(solution)/shard_map/dot_general | solution.py:38
  104.6 2.8 copy.10
  107.4 3.1 reshape.29
  110.5 4.0 %copy.11 = bf16[12,128,96,8]{1,3,2,0:T(8,128)(2,1)} copy(bf16[12,128,96,8]{1,0,3,2:T(8,128)(2,1)} %reshape.29) | data formatting | bytes 4718592
  114.5 103.4 %while.13 = (s32[]{:T(128)}, f32[96,8,256]{2,1,0:T(8,128)S(1)}, f32[96,256]{1,0:T(8,128)S(1)}, bf16[12,128,96,8]{1,3,2,0:T(8,128)(2,1)}, s32[12,128,96]{1,0,2:T(8,128)}, /*index=5*/s32[]{:T(128)}, s32[]{:T(128)}) while((s32[]{:T(128)}, f32[96,8,256]{2,1,0:T(8,128)S(1)}, f32[96,256]{1,0:T(8,128)S(1)}, ...), condition=%wide.region_6.7_spmd.clone, body=%wide.region_4.6_spmd.clone.sunk | while | flops 66478080 | bytes 2359900 | solution.py:60
  115.6 5.1 %fusion.23 = f32[96,8,256]{2,1,0:T(8,128)S(1)} fusion(s32[128,96]{0,1:T(8,128)S(1)} %bitcast.19, f32[96,8,256]{2,1,0:T(8,128)S(1)} %get-tuple-element.124, pred[]{:T(512)S(6)} %compare.3, bf16[12,128,96,8]{1,3,2,0:T(8,128)(2,1)} %get-tuple-element.133, s32[]{:T(128)} %get-tuple-element.123), kind=kOutput, calls=%fused_computation.9.clone.1 | convolution fusion | flops 53870592 | bytes 1819137 | tf_op jit(solution)/shard_map/while/body/eval_jaxpr/pmd,pmk->mdk/dot_general | solution.py:50
  120.6 2.5 convert_reduce_fusion.2
  124.2 5.1 %fusion.23 = f32[96,8,256]{2,1,0:T(8,128)S(1)} fusion(s32[128,96]{0,1:T(8,128)S(1)} %bitcast.19, f32[96,8,256]{2,1,0:T(8,128)S(1)} %get-tuple-element.124, pred[]{:T(512)S(6)} %compare.3, bf16[12,128,96,8]{1,3,2,0:T(8,128)(2,1)} %get-tuple-element.133, s32[]{:T(128)} %get-tuple-element.123), kind=kOutput, calls=%fused_computation.9.clone.1 | convolution fusion | flops 53870592 | bytes 1819137 | tf_op jit(solution)/shard_map/while/body/eval_jaxpr/pmd,pmk->mdk/dot_general | solution.py:50
  132.8 5.1 %fusion.23 = f32[96,8,256]{2,1,0:T(8,128)S(1)} fusion(s32[128,96]{0,1:T(8,128)S(1)} %bitcast.19, f32[96,8,256]{2,1,0:T(8,128)S(1)} %get-tuple-element.124, pred[]{:T(512)S(6)} %compare.3, bf16[12,128,96,8]{1,3,2,0:T(8,128)(2,1)} %get-tuple-element.133, s32[]{:T(128)} %get-tuple-element.123), kind=kOutput, calls=%fused_computation.9.clone.1 | convolution fusion | flops 53870592 | bytes 1819137 | tf_op jit(solution)/shard_map/while/body/eval_jaxpr/pmd,pmk->mdk/dot_general | solution.py:50
  141.4 5.1 %fusion.23 = f32[96,8,256]{2,1,0:T(8,128)S(1)} fusion(s32[128,96]{0,1:T(8,128)S(1)} %bitcast.19, f32[96,8,256]{2,1,0:T(8,128)S(1)} %get-tuple-element.124, pred[]{:T(512)S(6)} %compare.3, bf16[12,128,96,8]{1,3,2,0:T(8,128)(2,1)} %get-tuple-element.133, s32[]{:T(128)} %get-tuple-element.123), kind=kOutput, calls=%fused_computation.9.clone.1 | convolution fusion | flops 53870592 | bytes 1819137 | tf_op jit(solution)/shard_map/while/body/eval_jaxpr/pmd,pmk->mdk/dot_general | solution.py:50
  150.0 5.1 %fusion.23 = f32[96,8,256]{2,1,0:T(8,128)S(1)} fusion(s32[128,96]{0,1:T(8,128)S(1)} %bitcast.19, f32[96,8,256]{2,1,0:T(8,128)S(1)} %get-tuple-element.124, pred[]{:T(512)S(6)} %compare.3, bf16[12,128,96,8]{1,3,2,0:T(8,128)(2,1)} %get-tuple-element.133, s32[]{:T(128)} %get-tuple-element.123), kind=kOutput, calls=%fused_computation.9.clone.1 | convolution fusion | flops 53870592 | bytes 1819137 | tf_op jit(solution)/shard_map/while/body/eval_jaxpr/pmd,pmk->mdk/dot_general | solution.py:50
  158.7 5.1 %fusion.23 = f32[96,8,256]{2,1,0:T(8,128)S(1)} fusion(s32[128,96]{0,1:T(8,128)S(1)} %bitcast.19, f32[96,8,256]{2,1,0:T(8,128)S(1)} %get-tuple-element.124, pred[]{:T(512)S(6)} %compare.3, bf16[12,128,96,8]{1,3,2,0:T(8,128)(2,1)} %get-tuple-element.133, s32[]{:T(128)} %get-tuple-element.123), kind=kOutput, calls=%fused_computation.9.clone.1 | convolution fusion | flops 53870592 | bytes 1819137 | tf_op jit(solution)/shard_map/while/body/eval_jaxpr/pmd,pmk->mdk/dot_general | solution.py:50
  167.3 5.1 %fusion.23 = f32[96,8,256]{2,1,0:T(8,128)S(1)} fusion(s32[128,96]{0,1:T(8,128)S(1)} %bitcast.19, f32[96,8,256]{2,1,0:T(8,128)S(1)} %get-tuple-element.124, pred[]{:T(512)S(6)} %compare.3, bf16[12,128,96,8]{1,3,2,0:T(8,128)(2,1)} %get-tuple-element.133, s32[]{:T(128)} %get-tuple-element.123), kind=kOutput, calls=%fused_computation.9.clone.1 | convolution fusion | flops 53870592 | bytes 1819137 | tf_op jit(solution)/shard_map/while/body/eval_jaxpr/pmd,pmk->mdk/dot_general | solution.py:50
  175.9 5.1 %fusion.23 = f32[96,8,256]{2,1,0:T(8,128)S(1)} fusion(s32[128,96]{0,1:T(8,128)S(1)} %bitcast.19, f32[96,8,256]{2,1,0:T(8,128)S(1)} %get-tuple-element.124, pred[]{:T(512)S(6)} %compare.3, bf16[12,128,96,8]{1,3,2,0:T(8,128)(2,1)} %get-tuple-element.133, s32[]{:T(128)} %get-tuple-element.123), kind=kOutput, calls=%fused_computation.9.clone.1 | convolution fusion | flops 53870592 | bytes 1819137 | tf_op jit(solution)/shard_map/while/body/eval_jaxpr/pmd,pmk->mdk/dot_general | solution.py:50
  184.5 5.1 %fusion.23 = f32[96,8,256]{2,1,0:T(8,128)S(1)} fusion(s32[128,96]{0,1:T(8,128)S(1)} %bitcast.19, f32[96,8,256]{2,1,0:T(8,128)S(1)} %get-tuple-element.124, pred[]{:T(512)S(6)} %compare.3, bf16[12,128,96,8]{1,3,2,0:T(8,128)(2,1)} %get-tuple-element.133, s32[]{:T(128)} %get-tuple-element.123), kind=kOutput, calls=%fused_computation.9.clone.1 | convolution fusion | flops 53870592 | bytes 1819137 | tf_op jit(solution)/shard_map/while/body/eval_jaxpr/pmd,pmk->mdk/dot_general | solution.py:50
  193.1 5.1 %fusion.23 = f32[96,8,256]{2,1,0:T(8,128)S(1)} fusion(s32[128,96]{0,1:T(8,128)S(1)} %bitcast.19, f32[96,8,256]{2,1,0:T(8,128)S(1)} %get-tuple-element.124, pred[]{:T(512)S(6)} %compare.3, bf16[12,128,96,8]{1,3,2,0:T(8,128)(2,1)} %get-tuple-element.133, s32[]{:T(128)} %get-tuple-element.123), kind=kOutput, calls=%fused_computation.9.clone.1 | convolution fusion | flops 53870592 | bytes 1819137 | tf_op jit(solution)/shard_map/while/body/eval_jaxpr/pmd,pmk->mdk/dot_general | solution.py:50
  201.8 5.1 %fusion.23 = f32[96,8,256]{2,1,0:T(8,128)S(1)} fusion(s32[128,96]{0,1:T(8,128)S(1)} %bitcast.19, f32[96,8,256]{2,1,0:T(8,128)S(1)} %get-tuple-element.124, pred[]{:T(512)S(6)} %compare.3, bf16[12,128,96,8]{1,3,2,0:T(8,128)(2,1)} %get-tuple-element.133, s32[]{:T(128)} %get-tuple-element.123), kind=kOutput, calls=%fused_computation.9.clone.1 | convolution fusion | flops 53870592 | bytes 1819137 | tf_op jit(solution)/shard_map/while/body/eval_jaxpr/pmd,pmk->mdk/dot_general | solution.py:50
  210.4 5.1 %fusion.23 = f32[96,8,256]{2,1,0:T(8,128)S(1)} fusion(s32[128,96]{0,1:T(8,128)S(1)} %bitcast.19, f32[96,8,256]{2,1,0:T(8,128)S(1)} %get-tuple-element.124, pred[]{:T(512)S(6)} %compare.3, bf16[12,128,96,8]{1,3,2,0:T(8,128)(2,1)} %get-tuple-element.133, s32[]{:T(128)} %get-tuple-element.123), kind=kOutput, calls=%fused_computation.9.clone.1 | convolution fusion | flops 53870592 | bytes 1819137 | tf_op jit(solution)/shard_map/while/body/eval_jaxpr/pmd,pmk->mdk/dot_general | solution.py:50
  220.3 126.8 %all-reduce.9.cloned.1.call-done = (f32[768,256]{1,0:T(8,128)}, f32[96,256]{1,0:T(8,128)}) async-done(((f32[768,256]{1,0:T(8,128)}, f32[96,256]{1,0:T(8,128)}), (f32[768,256]{1,0:T(8,128)}, f32[96,256]{1,0:T(8,128)})) %all-reduce.9.cloned.1.call-update) | async-done | bytes 884752 | tf_op jit(solution)/shard_map/psum | solution.py:68
  (74 shorter events, 57.2 us)
Async XLA Ops:
  7.2 91.4 %copy-start = (bf16[768,768]{1,0:T(8,128)(2,1)S(1)}, bf16[768,768]{1,0:T(8,128)(2,1)}, u32[]{:S(2)}) copy-start(bf16[768,768]{1,0:T(8,128)(2,1)} %param.15) | copy-start | bytes 3538948
  7.2 44.9 %copy-start.6 = (s32[1536]{0:T(1024)S(1)}, s32[1536]{0:T(1024)}, u32[]{:S(2)}) copy-start(s32[1536]{0:T(1024)} %param.13) | copy-start | bytes 18436
  7.2 43.8 %copy-start.5 = (s32[1536,96]{0,1:T(8,128)S(1)}, s32[1536,96]{0,1:T(8,128)}, u32[]{:S(2)}) copy-start(s32[1536,96]{0,1:T(8,128)} %param.14) | copy-start | bytes 1769476
  7.2 83.8 %all-reduce.7.cloned.1.call-start = ((), (), s32[]{:S(2)}) async-start(), calls=%async_computation | async-start | bytes 786432 | tf_op jit(solution)/shard_map/psum | solution.py:30
  35.0 312.1 %all-reduce.9.cloned.1.call-start = ((), (), s32[]{:S(2)}) async-start(), calls=%async_computation.1 | async-start | bytes 1769472 | tf_op jit(solution)/shard_map/psum | solution.py:68
  110.5 4.0 %copy-start.1 = (f32[96,256]{1,0:T(8,128)S(1)}, f32[96,256]{1,0:T(8,128)}, u32[]{:S(2)}) copy-start(f32[96,256]{1,0:T(8,128)} %custom-call.1) | copy-start | bytes 294916
  110.5 4.0 %copy-start.3 = (f32[96,8,256]{2,1,0:T(8,128)S(1)}, f32[96,8,256]{2,1,0:T(8,128)}, u32[]{:S(2)}) copy-start(f32[96,8,256]{2,1,0:T(8,128)} %custom-call) | copy-start | bytes 2359300
  217.9 0.6 copy-start.2
  218.0 0.9 copy-start.4
Sparse Core Ops, SparseCore 0:
  35.1 55.8 all-reduce.6
  219.0 128.0 all-reduce.8
where the time goes:
time: 362 us; the launch traced here: 357 us
  waiting for transfers between devices  166 us (46%)
  matrix products  66.6 us (18%)
  other arithmetic  42.5 us (12%)
  blocking collectives  34.1 us (9%)
  local copies, waits for them, and re-layouts  32.6 us (9%)
  between operations  14.8 us (4%)
    psum x1, waiting for transfers between devices, body(): lax.psum((code_sums.reshape(feature_width, CODEWORDS), code_counts), ('li...  127 us
    dot_general x12, matrix products, accumulate(): jnp.einsum('pmd,pmk->mdk', rot_blk, onehot, preferred_element_type=jnp.fl...  60.6 us
    psum x1, waiting for transfers between devices, body(): total_sum, total_mass = lax.psum((partial_sum, partial_mass), 'points')  39 us
    reduce_sum x12, other arithmetic, accumulate(): code_counts = code_counts + jnp.sum(onehot, axis=0, dtype=jnp.float32)  29.6 us
    psum x1, blocking collectives, body(): total_sum, total_mass = lax.psum((partial_sum, partial_mass), 'points')  13.8 us
    dynamic_slice x12, local copies, waits for them, and re-layouts, body(): lax.scan(accumulate, initial, (rotated.reshape(block_count, block_rows, s...  12.4 us
    unnamed x1, blocking collectives  11.3 us
    all_gather x1, blocking collectives, body(): lax.all_gather(weighted, 'lists', axis=0, tiled=True)  9.01 us
  transfers between devices with their start and end apart: 2, of which 2 were waited for; matrix products, arithmetic and copies ran while one was open for 1% of the time, Pallas kernels for 0%

commit v1 on v0

--- a/solution.py
+++ b/solution.py
@@ -1,9 +1,18 @@
+import functools
 import jax
 import jax.numpy as jnp
 from jax import lax
 from jax.sharding import PartitionSpec as P
 
 CODEWORDS = 256
+
+
+def run_the_stacks_all(mine_x, mesh_dim, mesh_ax):
+    even = lax.psum(mine_x, axis_name=mesh_dim)
+    return lax.psum(even, mesh_ax)
+
+
+manage_chains_on = functools.partial(run_the_stacks_all, mesh_dim="points", mesh_ax="lists")
 
 
 def body(child_centroids, child_sizes, parent_of, points, assign, codes, rotation):
@@ -65,8 +74,8 @@
             codes.reshape(block_count, block_rows, subspaces),
         ),
     )
-    total_sums, total_counts = lax.psum(
-        (code_sums.reshape(feature_width, CODEWORDS), code_counts), ("lists", "points")
+    total_sums, total_counts = manage_chains_on(
+        (code_sums.reshape(feature_width, CODEWORDS), code_counts)
     )
     means = total_sums.reshape(subspaces, sub_width, CODEWORDS) / (1.0 + total_counts[:, None, :])
     return (merged, means.reshape(feature_width, CODEWORDS))

time: 362 us -> 344 us (0.950)
  waiting for transfers between devices: 166 us -> 147 us
    psum x1 -> x2, waiting for transfers between devices: 127 us -> 108 us  [the longest x1 56.4 us: run_the_stacks_all(): even = lax.psum(mine_x, axis_name=mesh_dim)]
  transfers between devices with their start and end apart: 2 -> 3, of which waited for: 2 -> 3; matrix products, arithmetic and copies ran while one was open for 1% -> 1% of each run, Pallas kernels for 0% -> 0%
where the time goes in v1:
time: 344 us; the launch traced here: 338 us
  waiting for transfers between devices  147 us (43%)
  matrix products  66.7 us (19%)
  other arithmetic  42.5 us (12%)
  blocking collectives  34.1 us (10%)
  local copies, waits for them, and re-layouts  32.6 us (9%)
  between operations  14.5 us (4%)
    dot_general x12, matrix products, accumulate(): jnp.einsum('pmd,pmk->mdk', rot_blk, onehot, preferred_element_type=jnp.fl...  60.6 us
    psum x1, waiting for transfers between devices, run_the_stacks_all(): even = lax.psum(mine_x, axis_name=mesh_dim)  56.4 us
    psum x1, waiting for transfers between devices, run_the_stacks_all(): return lax.psum(even, mesh_ax)  52 us
    psum x1, waiting for transfers between devices, body(): total_sum, total_mass = lax.psum((partial_sum, partial_mass), 'points')  39 us
    reduce_sum x12, other arithmetic, accumulate(): code_counts = code_counts + jnp.sum(onehot, axis=0, dtype=jnp.float32)  29.6 us
    psum x1, blocking collectives, body(): total_sum, total_mass = lax.psum((partial_sum, partial_mass), 'points')  13.8 us
    dynamic_slice x12, local copies, waits for them, and re-layouts, body(): lax.scan(accumulate, initial, (rotated.reshape(block_count, block_rows, s...  12.4 us
    unnamed x1, blocking collectives  11.3 us
  transfers between devices with their start and end apart: 3, of which 3 were waited for; matrix products, arithmetic and copies ran while one was open for 1% of the time, Pallas kernels for 0%

profile of v1, /device:TPU:0, one launch (start us, length us, event | category | flops | bytes accessed | tf_op | source)
XLA Modules:
  0.0 338.4 jit_solution(5957835746227253526)
XLA Ops:
  11.5 11.3 %all-reduce.3 = (f32[128]{0:T(128)S(1)}, f32[128]{0:T(128)S(1)}) all-reduce(f32[128]{0:T(128)S(1)} %convert_dynamic-update-slice_fusion, f32[128]{0:T(128)S(1)} %convert_dynamic-update-slice_fusion.1), channel_id=1, replica_groups=mesh['lists'=4,'points'=8] {'lists'}, use_global_device_ids=true, to_apply=%add | all-reduce | flops 256 | bytes 2048
  23.8 9.0 %all_gather.10 = f32[128,768]{1,0:T(8,128)S(1)} all-gather(f32[32,768]{1,0:T(8,128)S(1)} %broadcast_multiply_fusion), channel_id=1, replica_groups=mesh['lists'=4,'points'=8] {'lists'}, dimensions={0}, use_global_device_ids=true | all-gather | bytes 491520 | tf_op jit(solution)/shard_map/all_gather | solution.py:26
  36.5 13.8 %psum.43 = f32[128]{0:T(128)S(1)} all-reduce(f32[128]{0:T(128)S(1)} %scatter_custom_fusion.1), channel_id=1, replica_groups=mesh['lists'=4,'points'=8] {'points'}, use_global_device_ids=true, to_apply=%region_3.4 | all-reduce | flops 128 | bytes 1024 | tf_op jit(solution)/shard_map/psum | solution.py:39
  52.1 39.0 %all-reduce.9.cloned.1.call-done = f32[128,768]{1,0:T(8,128)} async-done(((f32[128,768]{1,0:T(8,128)}), f32[128,768]{1,0:T(8,128)}) %all-reduce.9.cloned.1.call-update) | async-done | bytes 393232 | tf_op jit(solution)/shard_map/psum | solution.py:39
  92.9 5.7 %gather_fusion = bf16[1536,768]{1,0:T(8,128)(2,1)} fusion(bf16[128,768]{1,0:T(8,128)(2,1)S(1)} %get-tuple-element.83, s32[2048]{0:T(1024)S(1)} %pad_clamp_fusion), kind=kCustom, calls=%fused_computation | custom fusion | bytes 4724736 | tf_op jit(solution)/shard_map/jit(_take)/gather | solution.py:45
  98.6 6.0 %convolution_convert_fusion = bf16[1536,768]{1,0:T(8,128)(2,1)} fusion(bf16[768,768]{1,0:T(8,128)(2,1)S(1)} %copy-done, bf16[1536,768]{1,0:T(8,128)(2,1)} %param.12, bf16[1536,768]{1,0:T(8,128)(2,1)} %gather_fusion, pred[1536]{0:T(1024)(128)(4,1)S(1)} %compare_and_fusion), kind=kOutput, calls=%fused_computation.16 | convolution fusion | flops 1819017216 | bytes 8259072 | tf_op jit(solution)/shard_map/dot_general | solution.py:47
  104.6 2.8 copy.10
  107.5 3.1 reshape.29
  110.5 4.0 %copy.11 = bf16[12,128,96,8]{1,3,2,0:T(8,128)(2,1)} copy(bf16[12,128,96,8]{1,0,3,2:T(8,128)(2,1)} %reshape.29) | data formatting | bytes 4718592
  114.5 103.4 %while.13 = (s32[]{:T(128)}, f32[96,8,256]{2,1,0:T(8,128)S(1)}, f32[96,256]{1,0:T(8,128)S(1)}, bf16[12,128,96,8]{1,3,2,0:T(8,128)(2,1)}, s32[12,128,96]{1,0,2:T(8,128)}, /*index=5*/s32[]{:T(128)}, s32[]{:T(128)}) while((s32[]{:T(128)}, f32[96,8,256]{2,1,0:T(8,128)S(1)}, f32[96,256]{1,0:T(8,128)S(1)}, ...), condition=%wide.region_6.7_spmd.clone, body=%wide.region_4.6_spmd.clone.sunk | while | flops 66478080 | bytes 2359900 | solution.py:69
  115.6 5.1 %fusion.23 = f32[96,8,256]{2,1,0:T(8,128)S(1)} fusion(s32[128,96]{0,1:T(8,128)S(1)} %bitcast.19, f32[96,8,256]{2,1,0:T(8,128)S(1)} %get-tuple-element.126, pred[]{:T(512)S(6)} %compare.3, bf16[12,128,96,8]{1,3,2,0:T(8,128)(2,1)} %get-tuple-element.135, s32[]{:T(128)} %get-tuple-element.125), kind=kOutput, calls=%fused_computation.9.clone.1 | convolution fusion | flops 53870592 | bytes 1819137 | tf_op jit(solution)/shard_map/while/body/eval_jaxpr/pmd,pmk->mdk/dot_general | solution.py:59
  124.2 5.1 %fusion.23 = f32[96,8,256]{2,1,0:T(8,128)S(1)} fusion(s32[128,96]{0,1:T(8,128)S(1)} %bitcast.19, f32[96,8,256]{2,1,0:T(8,128)S(1)} %get-tuple-element.126, pred[]{:T(512)S(6)} %compare.3, bf16[12,128,96,8]{1,3,2,0:T(8,128)(2,1)} %get-tuple-element.135, s32[]{:T(128)} %get-tuple-element.125), kind=kOutput, calls=%fused_computation.9.clone.1 | convolution fusion | flops 53870592 | bytes 1819137 | tf_op jit(solution)/shard_map/while/body/eval_jaxpr/pmd,pmk->mdk/dot_general | solution.py:59
  132.8 5.1 %fusion.23 = f32[96,8,256]{2,1,0:T(8,128)S(1)} fusion(s32[128,96]{0,1:T(8,128)S(1)} %bitcast.19, f32[96,8,256]{2,1,0:T(8,128)S(1)} %get-tuple-element.126, pred[]{:T(512)S(6)} %compare.3, bf16[12,128,96,8]{1,3,2,0:T(8,128)(2,1)} %get-tuple-element.135, s32[]{:T(128)} %get-tuple-element.125), kind=kOutput, calls=%fused_computation.9.clone.1 | convolution fusion | flops 53870592 | bytes 1819137 | tf_op jit(solution)/shard_map/while/body/eval_jaxpr/pmd,pmk->mdk/dot_general | solution.py:59
  141.4 5.1 %fusion.23 = f32[96,8,256]{2,1,0:T(8,128)S(1)} fusion(s32[128,96]{0,1:T(8,128)S(1)} %bitcast.19, f32[96,8,256]{2,1,0:T(8,128)S(1)} %get-tuple-element.126, pred[]{:T(512)S(6)} %compare.3, bf16[12,128,96,8]{1,3,2,0:T(8,128)(2,1)} %get-tuple-element.135, s32[]{:T(128)} %get-tuple-element.125), kind=kOutput, calls=%fused_computation.9.clone.1 | convolution fusion | flops 53870592 | bytes 1819137 | tf_op jit(solution)/shard_map/while/body/eval_jaxpr/pmd,pmk->mdk/dot_general | solution.py:59
  150.1 5.1 %fusion.23 = f32[96,8,256]{2,1,0:T(8,128)S(1)} fusion(s32[128,96]{0,1:T(8,128)S(1)} %bitcast.19, f32[96,8,256]{2,1,0:T(8,128)S(1)} %get-tuple-element.126, pred[]{:T(512)S(6)} %compare.3, bf16[12,128,96,8]{1,3,2,0:T(8,128)(2,1)} %get-tuple-element.135, s32[]{:T(128)} %get-tuple-element.125), kind=kOutput, calls=%fused_computation.9.clone.1 | convolution fusion | flops 53870592 | bytes 1819137 | tf_op jit(solution)/shard_map/while/body/eval_jaxpr/pmd,pmk->mdk/dot_general | solution.py:59
  158.7 5.1 %fusion.23 = f32[96,8,256]{2,1,0:T(8,128)S(1)} fusion(s32[128,96]{0,1:T(8,128)S(1)} %bitcast.19, f32[96,8,256]{2,1,0:T(8,128)S(1)} %get-tuple-element.126, pred[]{:T(512)S(6)} %compare.3, bf16[12,128,96,8]{1,3,2,0:T(8,128)(2,1)} %get-tuple-element.135, s32[]{:T(128)} %get-tuple-element.125), kind=kOutput, calls=%fused_computation.9.clone.1 | convolution fusion | flops 53870592 | bytes 1819137 | tf_op jit(solution)/shard_map/while/body/eval_jaxpr/pmd,pmk->mdk/dot_general | solution.py:59
  167.3 5.1 %fusion.23 = f32[96,8,256]{2,1,0:T(8,128)S(1)} fusion(s32[128,96]{0,1:T(8,128)S(1)} %bitcast.19, f32[96,8,256]{2,1,0:T(8,128)S(1)} %get-tuple-element.126, pred[]{:T(512)S(6)} %compare.3, bf16[12,128,96,8]{1,3,2,0:T(8,128)(2,1)} %get-tuple-element.135, s32[]{:T(128)} %get-tuple-element.125), kind=kOutput, calls=%fused_computation.9.clone.1 | convolution fusion | flops 53870592 | bytes 1819137 | tf_op jit(solution)/shard_map/while/body/eval_jaxpr/pmd,pmk->mdk/dot_general | solution.py:59
  175.9 5.1 %fusion.23 = f32[96,8,256]{2,1,0:T(8,128)S(1)} fusion(s32[128,96]{0,1:T(8,128)S(1)} %bitcast.19, f32[96,8,256]{2,1,0:T(8,128)S(1)} %get-tuple-element.126, pred[]{:T(512)S(6)} %compare.3, bf16[12,128,96,8]{1,3,2,0:T(8,128)(2,1)} %get-tuple-element.135, s32[]{:T(128)} %get-tuple-element.125), kind=kOutput, calls=%fused_computation.9.clone.1 | convolution fusion | flops 53870592 | bytes 1819137 | tf_op jit(solution)/shard_map/while/body/eval_jaxpr/pmd,pmk->mdk/dot_general | solution.py:59
  184.5 5.1 %fusion.23 = f32[96,8,256]{2,1,0:T(8,128)S(1)} fusion(s32[128,96]{0,1:T(8,128)S(1)} %bitcast.19, f32[96,8,256]{2,1,0:T(8,128)S(1)} %get-tuple-element.126, pred[]{:T(512)S(6)} %compare.3, bf16[12,128,96,8]{1,3,2,0:T(8,128)(2,1)} %get-tuple-element.135, s32[]{:T(128)} %get-tuple-element.125), kind=kOutput, calls=%fused_computation.9.clone.1 | convolution fusion | flops 53870592 | bytes 1819137 | tf_op jit(solution)/shard_map/while/body/eval_jaxpr/pmd,pmk->mdk/dot_general | solution.py:59
  193.1 5.1 %fusion.23 = f32[96,8,256]{2,1,0:T(8,128)S(1)} fusion(s32[128,96]{0,1:T(8,128)S(1)} %bitcast.19, f32[96,8,256]{2,1,0:T(8,128)S(1)} %get-tuple-element.126, pred[]{:T(512)S(6)} %compare.3, bf16[12,128,96,8]{1,3,2,0:T(8,128)(2,1)} %get-tuple-element.135, s32[]{:T(128)} %get-tuple-element.125), kind=kOutput, calls=%fused_computation.9.clone.1 | convolution fusion | flops 53870592 | bytes 1819137 | tf_op jit(solution)/shard_map/while/body/eval_jaxpr/pmd,pmk->mdk/dot_general | solution.py:59
  201.8 5.1 %fusion.23 = f32[96,8,256]{2,1,0:T(8,128)S(1)} fusion(s32[128,96]{0,1:T(8,128)S(1)} %bitcast.19, f32[96,8,256]{2,1,0:T(8,128)S(1)} %get-tuple-element.126, pred[]{:T(512)S(6)} %compare.3, bf16[12,128,96,8]{1,3,2,0:T(8,128)(2,1)} %get-tuple-element.135, s32[]{:T(128)} %get-tuple-element.125), kind=kOutput, calls=%fused_computation.9.clone.1 | convolution fusion | flops 53870592 | bytes 1819137 | tf_op jit(solution)/shard_map/while/body/eval_jaxpr/pmd,pmk->mdk/dot_general | solution.py:59
  210.4 5.1 %fusion.23 = f32[96,8,256]{2,1,0:T(8,128)S(1)} fusion(s32[128,96]{0,1:T(8,128)S(1)} %bitcast.19, f32[96,8,256]{2,1,0:T(8,128)S(1)} %get-tuple-element.126, pred[]{:T(512)S(6)} %compare.3, bf16[12,128,96,8]{1,3,2,0:T(8,128)(2,1)} %get-tuple-element.135, s32[]{:T(128)} %get-tuple-element.125), kind=kOutput, calls=%fused_computation.9.clone.1 | convolution fusion | flops 53870592 | bytes 1819137 | tf_op jit(solution)/shard_map/while/body/eval_jaxpr/pmd,pmk->mdk/dot_general | solution.py:59
  218.9 56.4 %all-reduce.11.cloned.1.call-done = (f32[768,256]{1,0:T(8,128)}, f32[96,256]{1,0:T(8,128)}) async-done(((f32[768,256]{1,0:T(8,128)}, f32[96,256]{1,0:T(8,128)}), (f32[768,256]{1,0:T(8,128)}, f32[96,256]{1,0:T(8,128)})) %all-reduce.11.cloned.1.call-update) | async-done | bytes 884752 | tf_op jit(solution)/shard_map/psum | solution.py:11
  276.8 52.0 %all-reduce.13.cloned.1.call-done = (f32[768,256]{1,0:T(8,128)}, f32[96,256]{1,0:T(8,128)}) async-done(((f32[768,256]{1,0:T(8,128)}, f32[96,256]{1,0:T(8,128)}), (f32[768,256]{1,0:T(8,128)}, f32[96,256]{1,0:T(8,128)})) %all-reduce.13.cloned.1.call-update) | async-done | bytes 884752 | tf_op jit(solution)/shard_map/psum | solution.py:12
  (77 shorter events, 59.7 us)
Async XLA Ops:
  7.2 91.4 %copy-start = (bf16[768,768]{1,0:T(8,128)(2,1)S(1)}, bf16[768,768]{1,0:T(8,128)(2,1)}, u32[]{:S(2)}) copy-start(bf16[768,768]{1,0:T(8,128)(2,1)} %param.15) | copy-start | bytes 3538948
  7.2 44.9 %copy-start.6 = (s32[1536]{0:T(1024)S(1)}, s32[1536]{0:T(1024)}, u32[]{:S(2)}) copy-start(s32[1536]{0:T(1024)} %param.13) | copy-start | bytes 18436
  7.2 43.8 %copy-start.5 = (s32[1536,96]{0,1:T(8,128)S(1)}, s32[1536,96]{0,1:T(8,128)}, u32[]{:S(2)}) copy-start(s32[1536,96]{0,1:T(8,128)} %param.14) | copy-start | bytes 1769476
  7.2 83.8 %all-reduce.9.cloned.1.call-start = ((), (), s32[]{:S(2)}) async-start(), calls=%async_computation | async-start | bytes 786432 | tf_op jit(solution)/shard_map/psum | solution.py:39
  35.0 240.4 %all-reduce.11.cloned.1.call-start = ((), (), s32[]{:S(2)}) async-start(), calls=%async_computation.1 | async-start | bytes 1769472 | tf_op jit(solution)/shard_map/psum | solution.py:11
  110.5 4.0 %copy-start.1 = (f32[96,256]{1,0:T(8,128)S(1)}, f32[96,256]{1,0:T(8,128)}, u32[]{:S(2)}) copy-start(f32[96,256]{1,0:T(8,128)} %custom-call.1) | copy-start | bytes 294916
  110.5 4.0 %copy-start.3 = (f32[96,8,256]{2,1,0:T(8,128)S(1)}, f32[96,8,256]{2,1,0:T(8,128)}, u32[]{:S(2)}) copy-start(f32[96,8,256]{2,1,0:T(8,128)} %custom-call) | copy-start | bytes 2359300
  218.0 0.6 copy-start.2
  218.0 0.9 copy-start.4
  218.9 110.0 %all-reduce.13.cloned.1.call-start = ((), (), s32[]{:S(2)}) async-start(), calls=%async_computation.2 | async-start | bytes 1769472 | tf_op jit(solution)/shard_map/psum | solution.py:12
Sparse Core Ops, SparseCore 0:
  35.2 55.8 all-reduce.8
  219.0 56.3 all-reduce.10
  278.5 50.2 all-reduce.12
